TPU v7x, 32 devices: a whole 2x2x4 slice. The times are simulated.
32 devices in a mesh: expert: 8 (over y, x, core), dp: 4 (over z).
Axes of the slice: x: 2, y: 2, z: 4, core: 2. Of those that a mesh axis runs over, the one named last changes fastest.
Arguments:
- tokens: bfloat16 [4096, 2048], P(('expert', 'dp')), may hold values from -6 to 6
- expert_ids: int32 [4096, 8], P(('expert', 'dp')), may hold values from 0 to 15, all different within a row; in each aligned block of 128 rows (0 to 127, 128 to 255, ...) at most 72 rows name the same one
- router: bfloat16 [2048, 16], replicated, may hold values from -0.25 to 0.25
- w_gate: bfloat16 [16, 2048, 640], P('expert'), may hold values from -0.125 to 0.125
- w_up: bfloat16 [16, 2048, 640], P('expert'), may hold values from -0.125 to 0.125
- w_down: bfloat16 [16, 640, 2048], P('expert'), may hold values from -1 to 1
- out_grad: bfloat16 [4096, 2048], P(('expert', 'dp')), may hold values from -6 to 6
Outputs:
- mixed: bfloat16 [4096, 2048], P(('expert', 'dp'))
- token_grad: bfloat16 [4096, 2048], P(('expert', 'dp'))
- router_grad: float32 [2048, 16], replicated
- gate_grad: bfloat16 [16, 2048, 640], P('expert', 'dp')
- up_grad: bfloat16 [16, 2048, 640], P('expert', 'dp')
- down_grad: bfloat16 [16, 640, 2048], P('expert', None, 'dp')
Inputs may be any that keep to these rules, and one draw needn't show every extreme that they name: `expert_ids`: each row names 8 different experts; within the 128 rows of one device no expert is named more than 72 times.
All inputs are finite; a program needn't handle non-finite values.
Results may differ from a plain program's by a relative error of at most 0.008.
Values may be sent and summed in bfloat16 or wider, within the bound.
No kernel may reach another device: no remote copies, remote signals or barrier semaphores. Data moves between devices by JAX's collectives and lax.ppermute only.
A program may use at most 256 MiB of HBM per device.

v0:
```python
import jax
import jax.numpy as jnp
from jax import lax
from jax.sharding import PartitionSpec as P


def flat_rows(array):
    return array.reshape(array.shape[0], array.shape[1] * array.shape[2], array.shape[3])


def body(tokens, expert_ids, router, w_gate, w_up, w_down, out_grad):
    f32 = jnp.float32
    bf16 = jnp.bfloat16
    tok_dev, width = tokens.shape
    top = expert_ids.shape[1]
    n_experts = router.shape[1]
    local_experts = w_gate.shape[0]
    groups = lax.axis_size("expert")
    capacity = (tok_dev * top * 9 + 8 * n_experts - 1) // (8 * n_experts)
    n_assign = tok_dev * top
    flat_ids = expert_ids.reshape(-1)
    ladder = jnp.arange(n_experts, dtype=jnp.int32)
    onehot = (flat_ids[:, None] == ladder[None, :]).astype(jnp.int32)
    rank = jnp.sum((jnp.cumsum(onehot, axis=0) - onehot) * onehot, axis=1)
    owner = flat_ids // local_experts
    within = flat_ids % local_experts
    dest = (within * groups + owner) * capacity + rank
    slot_src = jnp.full((n_experts * capacity,), n_assign, jnp.int32)
    slot_src = slot_src.at[dest].set(jnp.arange(n_assign, dtype=jnp.int32))
    live = slot_src < n_assign
    slot_tok = jnp.where(live, slot_src // top, 0)
    logits = jnp.dot(tokens, router, preferred_element_type=f32)
    scores = jax.nn.sigmoid(logits)
    chosen = jnp.take_along_axis(scores, expert_ids, axis=1)
    total = jnp.sum(chosen, axis=1, keepdims=True)
    gates = chosen / total
    gate_slots = jnp.where(live, gates.reshape(-1)[jnp.minimum(slot_src, n_assign - 1)], 0.0)
    send = jnp.where(live[:, None], tokens[slot_tok], jnp.zeros((), bf16))
    send = send.reshape(local_experts, groups, capacity, width)
    piece = lax.all_to_all(send, "expert", split_axis=1, concat_axis=1, tiled=True)
    shape = piece.shape
    rows = flat_rows(piece)
    pre_gate = jnp.einsum("jrd,jdf->jrf", rows, w_gate, preferred_element_type=f32)
    pre_up = jnp.einsum("jrd,jdf->jrf", rows, w_up, preferred_element_type=f32)
    hidden = (pre_gate * jax.nn.sigmoid(pre_gate) * pre_up).astype(bf16)
    expert_out = jnp.einsum("jrf,jfd->jrd", hidden, w_down, preferred_element_type=f32).astype(bf16)
    hid_shape = (shape[0], shape[1], shape[2], hidden.shape[2])
    expert_out = expert_out.reshape(shape)
    hidden = hidden.reshape(hid_shape)
    results = (expert_out, hidden, piece, pre_gate.reshape(hid_shape), pre_up.reshape(hid_shape))
    expert_out = results[0]
    hidden = flat_rows(results[1])
    back = lax.all_to_all(expert_out, "expert", split_axis=1, concat_axis=1, tiled=True).reshape(
        n_experts * capacity, width
    )
    picked = back[dest].reshape(tok_dev, top, width)
    mixed = jnp.einsum("tk,tkd->td", gates, picked.astype(f32)).astype(bf16)
    gate_sens = jnp.einsum("tkd,td->tk", picked, out_grad, preferred_element_type=f32)
    grad_rows = (gate_slots[:, None] * out_grad[slot_tok].astype(f32)).astype(bf16)
    grad_send = jnp.where(live[:, None], grad_rows, jnp.zeros((), bf16))
    grad_send = grad_send.reshape(local_experts, groups, capacity, width)
    grad_in4 = lax.all_to_all(grad_send, "expert", split_axis=1, concat_axis=1, tiled=True)
    grad_in = flat_rows(grad_in4)
    pre_gate = flat_rows(results[3])
    pre_up = flat_rows(results[4])
    hidden_grad = jnp.einsum("jrd,jfd->jrf", grad_in, w_down, preferred_element_type=f32)
    sig = jax.nn.sigmoid(pre_gate)
    silu_val = pre_gate * sig
    gate_term = (hidden_grad * pre_up * sig * (1.0 + pre_gate * (1.0 - sig))).astype(bf16)
    up_term = (hidden_grad * silu_val).astype(bf16)
    input_grad = (
        jnp.einsum("jrf,jdf->jrd", gate_term, w_gate, preferred_element_type=f32)
        + jnp.einsum("jrf,jdf->jrd", up_term, w_up, preferred_element_type=f32)
    ).astype(bf16)
    input_grad = input_grad.reshape(grad_in4.shape)
    returned = lax.all_to_all(
        input_grad, "expert", split_axis=1, concat_axis=1, tiled=True
    ).reshape(n_experts * capacity, width)
    moe_grad = jnp.sum(returned[dest].reshape(tok_dev, top, width).astype(f32), axis=1)
    chosen_grad = (gate_sens - jnp.sum(gate_sens * gates, axis=1, keepdims=True)) / total
    sel_grad = chosen_grad * chosen * (1.0 - chosen)
    pick = (expert_ids[:, :, None] == ladder[None, None, :]).astype(f32)
    logit_grad = jnp.einsum("tk,tke->te", sel_grad, pick).astype(bf16)
    token_grad = (moe_grad + jnp.dot(logit_grad, router.T, preferred_element_type=f32)).astype(bf16)
    router_grad = lax.psum(
        jnp.dot(tokens.T, logit_grad, preferred_element_type=f32), ("expert", "dp")
    )
    hidden_width = hidden.shape[2]
    arrived4 = results[2]
    columns = (
        lax.all_to_all(arrived4, "dp", split_axis=3, concat_axis=1, tiled=True),
        lax.all_to_all(grad_in4, "dp", split_axis=3, concat_axis=1, tiled=True),
    )
    hid_shape = (local_experts, groups, capacity, hidden_width)
    hiddens = (
        lax.all_gather(gate_term.reshape(hid_shape), "dp", axis=1, tiled=True),
        lax.all_gather(up_term.reshape(hid_shape), "dp", axis=1, tiled=True),
        lax.all_gather(results[1], "dp", axis=1, tiled=True),
    )
    x_cols = flat_rows(columns[0])
    g_cols = flat_rows(columns[1])
    gate_grad = jnp.einsum(
        "jrd,jrf->jdf", x_cols, flat_rows(hiddens[0]), preferred_element_type=f32
    ).astype(bf16)
    up_grad = jnp.einsum(
        "jrd,jrf->jdf", x_cols, flat_rows(hiddens[1]), preferred_element_type=f32
    ).astype(bf16)
    down_grad = jnp.einsum(
        "jrf,jrd->jfd", flat_rows(hiddens[2]), g_cols, preferred_element_type=f32
    ).astype(bf16)
    return (mixed, token_grad, router_grad, gate_grad, up_grad, down_grad)


def solution(mesh):
    placed = (
        P(("expert", "dp"), None),
        P(("expert", "dp"), None),
        P(),
        P("expert", None, None),
        P("expert", None, None),
        P("expert", None, None),
        P(("expert", "dp"), None),
    )
    return jax.shard_map(
        body,
        mesh=mesh,
        in_specs=placed,
        out_specs=(
            P(("expert", "dp"), None),
            P(("expert", "dp"), None),
            P(),
            P("expert", "dp", None),
            P("expert", "dp", None),
            P("expert", None, "dp"),
        ),
        check_vma=False,
    )
```

profile of v0, /device:TPU:0, one launch (start us, length us, event | category | flops | bytes accessed | tf_op | source)
XLA Modules:
  0.0 936.1 jit_solution(13658574191496700082)
XLA Ops:
  18.7 6.0 gather_fusion
  27.4 59.9 %all_to_all.50 = bf16[2,8,72,2048]{3,2,0,1:T(8,128)(2,1)S(1)} all-to-all(bf16[2,8,72,2048]{3,2,0,1:T(8,128)(2,1)S(1)} %copy_select_fusion), channel_id=1, replica_groups=mesh['expert'=8,'dp'=4] {'expert'}, dimensions={1} | all-to-all | bytes 9437184 | tf_op jit(solution)/shard_map/all_to_all | solution.py:40
  93.6 5.7 multiply_convert_fusion.2
  111.9 7.0 gather_fusion.5
  119.1 5.9 gather_fusion.3
  125.1 40.4 %all-to-all-done.1 = bf16[2,8,72,2048]{3,2,0,1:T(8,128)(2,1)} async-done(((bf16[2,8,72,2048]{3,2,0,1:T(8,128)(2,1)}), bf16[2,8,72,2048]{3,2,0,1:T(8,128)(2,1)}, u32[]{:S(2)}, u32[]{:S(2)}) %all-to-all-start.1) | async-done | bytes 4718624 | tf_op jit(solution)/shard_map/all_to_all | solution.py:53
  170.6 11.8 %gather_fusion.1 = bf16[1024,2048]{1,0:T(8,128)(2,1)} fusion(bf16[1152,2048]{1,0:T(8,128)(2,1)} %bitcast.104, s32[1024]{0:T(1024)S(1)} %broadcast_clamp_fusion), kind=kCustom, calls=%fused_computation.1 | custom fusion | bytes 8392704 | tf_op jit(solution)/shard_map/gather | solution.py:56
  201.3 11.7 %copy.125 = bf16[2,8,72,2048]{2,1,0,3:T(8,128)(2,1)} copy(bf16[2,8,72,2048]{3,2,0,1:T(8,128)(2,1)} %copy-done.3) | data formatting | bytes 9437184 | tf_op jit(solution)/shard_map/all_to_all | solution.py:40
  213.0 43.1 %all-to-all-done.2 = bf16[2,8,72,2048]{3,2,0,1:T(8,128)(2,1)} async-done(((bf16[2,8,72,2048]{3,2,0,1:T(8,128)(2,1)}), bf16[2,8,72,2048]{3,2,0,1:T(8,128)(2,1)}, u32[]{:S(2)}, u32[]{:S(2)}) %all-to-all-start.2) | async-done | bytes 4718624 | tf_op jit(solution)/shard_map/all_to_all | solution.py:62
  266.1 8.5 multiply_convert_fusion
  274.6 11.3 %fusion.34 = f32[2,576,2048]{2,1,0:T(8,128)} fusion(bf16[2,576,640]{2,1,0:T(8,128)(2,1)} %get-tuple-element.11, bf16[2,2048,640]{2,1,0:T(8,128)(2,1)} %param.10), kind=kOutput, calls=%fused_computation.86 | convolution fusion | flops 3019898880 | bytes 16154624 | tf_op jit(solution)/shard_map/jrf,jdf->jrd/dot_general | solution.py:72
  285.9 8.1 add_convert_fusion
  296.5 240.4 %all-to-all-done.4 = bf16[2,8,72,2048]{2,1,0,3:T(8,128)(2,1)} async-done(((bf16[2,8,72,2048]{2,1,0,3:T(8,128)(2,1)}), bf16[2,8,72,2048]{2,1,0,3:T(8,128)(2,1)}, u32[]{:S(2)}, u32[]{:S(2)}) %all-to-all-start.4) | async-done | bytes 4718624 | tf_op jit(solution)/shard_map/all_to_all | solution.py:91
  542.6 11.8 %copy.130 = bf16[2,8,72,2048]{2,1,0,3:T(8,128)(2,1)} copy(bf16[2,8,72,2048]{3,2,0,1:T(8,128)(2,1)} %all-to-all-done.2) | data formatting | bytes 9437184 | tf_op jit(solution)/shard_map/all_to_all | solution.py:62
  554.4 42.3 %all-to-all-done.3 = bf16[2,8,72,2048]{3,2,0,1:T(8,128)(2,1)} async-done(((bf16[2,8,72,2048]{3,2,0,1:T(8,128)(2,1)}), bf16[2,8,72,2048]{3,2,0,1:T(8,128)(2,1)}, u32[]{:S(2)}, u32[]{:S(2)}) %all-to-all-start.3) | async-done | bytes 4718624 | tf_op jit(solution)/shard_map/all_to_all | solution.py:76
  596.7 5.6 all-to-all-start.5
  608.7 10.7 %copy.142 = bf16[2,8,72,4,512]{4,3,2,1,0:T(4,128)(2,1)} copy(bf16[2,8,72,4,512]{2,1,0,4,3:T(8,128)(2,1)} %bitcast.23) | data formatting | bytes 9437184 | tf_op jit(solution)/shard_map/all_to_all | solution.py:91
  630.2 11.8 %gather_fusion.4 = bf16[1024,2048]{1,0:T(8,128)(2,1)} fusion(bf16[1152,2048]{1,0:T(8,128)(2,1)} %bitcast.103, s32[1024]{0:T(1024)S(1)} %broadcast_clamp_fusion), kind=kCustom, calls=%fused_computation.4 | custom fusion | bytes 8392704 | tf_op jit(solution)/shard_map/gather | solution.py:79
  648.0 185.0 %all-to-all-done.5 = bf16[2,8,72,2048]{2,1,0,3:T(8,128)(2,1)} async-done(((bf16[2,8,72,2048]{2,1,0,3:T(8,128)(2,1)}), bf16[2,8,72,2048]{2,1,0,3:T(8,128)(2,1)}, u32[]{:S(2)}, u32[]{:S(2)}) %all-to-all-start.5) | async-done | bytes 4718624 | tf_op jit(solution)/shard_map/all_to_all | solution.py:92
  833.0 13.3 %copy.131 = bf16[2,8,72,4,512]{4,2,1,3,0:T(8,128)(2,1)} copy(bf16[2,8,72,4,512]{2,1,0,4,3:T(8,128)(2,1)} %bitcast.32) | data formatting | bytes 9437184 | tf_op jit(solution)/shard_map/all_to_all | solution.py:92
  846.4 8.4 convolution_convert_fusion.1
  854.8 9.1 convolution_convert_fusion.3
  863.9 9.2 convolution_convert_fusion.2
  873.1 53.9 %all-reduce.2.cloned.1.call-done = f32[2048,16]{0,1:T(8,128)} async-done(((f32[2048,16]{0,1:T(8,128)}), f32[2048,16]{0,1:T(8,128)}) %all-reduce.2.cloned.1.call-update) | async-done | bytes 131088 | tf_op jit(solution)/shard_map/psum | solution.py:85
  (114 shorter events, 99.2 us)
Async XLA Ops:
  8.0 111.1 %copy-start = (bf16[128,2048]{1,0:T(8,128)(2,1)S(1)}, bf16[128,2048]{1,0:T(8,128)(2,1)}, u32[]{:S(2)}) copy-start(bf16[128,2048]{1,0:T(8,128)(2,1)} %param.13) | copy-start | bytes 1572868
  8.0 10.7 %copy-start.2 = (bf16[128,2048]{1,0:T(8,128)(2,1)S(1)}, bf16[128,2048]{1,0:T(8,128)(2,1)}, u32[]{:S(2)}) copy-start(bf16[128,2048]{1,0:T(8,128)(2,1)} %param.7) | copy-start | bytes 1572868
  8.9 15.8 %copy-start.6 = (s32[128,8]{1,0:T(8,128)}, s32[128,8]{1,0:T(8,128)S(1)}, u32[]{:S(2)}) copy-start(s32[128,8]{1,0:T(8,128)S(1)} %copy.108) | copy-start | bytes 12292
  27.4 62.3 %slice-start.2 = ((s8[5242880]{0:T(1024)(128)(4,1)}), s8[4194304]{0:T(1024)(128)(4,1)S(1)}, s32[]{:S(2)}) async-start(s8[5242880]{0:T(1024)(128)(4,1)} %bitcast.133), calls=%async_computation.12 | async-start | bytes 8388608
  87.3 6.3 slice-start.4
  89.7 9.6 %slice-start = ((s8[5242880]{0:T(1024)(128)(4,1)}), s8[4194304]{0:T(1024)(128)(4,1)S(1)}, s32[]{:S(2)}) async-start(s8[5242880]{0:T(1024)(128)(4,1)} %bitcast.131), calls=%async_computation.10 | async-start | bytes 8388608
  93.6 5.7 copy-start.10
  93.6 5.7 slice-start.1
  99.3 4.1 copy-start.4
  106.0 5.5 copy-start.9
  106.0 5.7 copy-start.8
  106.0 59.5 %all-to-all-start.1 = ((bf16[2,8,72,2048]{3,2,0,1:T(8,128)(2,1)}), bf16[2,8,72,2048]{3,2,0,1:T(8,128)(2,1)}, u32[]{:S(2)}, u32[]{:S(2)}) async-start(bf16[2,8,72,2048]{3,2,0,1:T(8,128)(2,1)} %copy.116), calls=%async_computation.1 | async-start | bytes 9437184 | tf_op jit(solution)/shard_map/all_to_all | solution.py:53
  110.7 735.7 %all-gather.8.cloned.1.call-start = ((), (), s32[]{:S(2)}) async-start(), calls=%async_computation.9 | async-start | bytes 7372800 | tf_op jit(solution)/shard_map/all_gather | solution.py:98
  196.7 59.4 %all-to-all-start.2 = ((bf16[2,8,72,2048]{3,2,0,1:T(8,128)(2,1)}), bf16[2,8,72,2048]{3,2,0,1:T(8,128)(2,1)}, u32[]{:S(2)}, u32[]{:S(2)}) async-start(bf16[2,8,72,2048]{3,2,0,1:T(8,128)(2,1)} %fusion.1), calls=%async_computation.2 | async-start | bytes 9437184 | tf_op jit(solution)/shard_map/all_to_all | solution.py:62
  256.1 280.8 %all-to-all-start.4 = ((bf16[2,8,72,2048]{2,1,0,3:T(8,128)(2,1)}), bf16[2,8,72,2048]{2,1,0,3:T(8,128)(2,1)}, u32[]{:S(2)}, u32[]{:S(2)}) async-start(bf16[2,8,72,2048]{2,1,0,3:T(8,128)(2,1)} %copy.125), calls=%async_computation.4 | async-start | bytes 16777216 | tf_op jit(solution)/shard_map/all_to_all | solution.py:91
  261.7 593.1 %all-gather.4.cloned.1.call-start = ((), (), s32[]{:S(2)}) async-start(), calls=%async_computation.7 | async-start | bytes 7372800 | tf_op jit(solution)/shard_map/all_gather | solution.py:96
  261.9 4.1 copy-start.12
  274.5 11.3 %copy-start.5 = (bf16[2,576,640]{2,1,0:T(8,128)(2,1)}, bf16[2,576,640]{2,1,0:T(8,128)(2,1)S(1)}, u32[]{:S(2)}) copy-start(bf16[2,576,640]{2,1,0:T(8,128)(2,1)S(1)} %get-tuple-element.10) | copy-start | bytes 4423684
  536.9 59.8 %all-to-all-start.3 = ((bf16[2,8,72,2048]{3,2,0,1:T(8,128)(2,1)}), bf16[2,8,72,2048]{3,2,0,1:T(8,128)(2,1)}, u32[]{:S(2)}, u32[]{:S(2)}) async-start(bf16[2,8,72,2048]{3,2,0,1:T(8,128)(2,1)} %copy.122), calls=%async_computation.3 | async-start | bytes 9437184 | tf_op jit(solution)/shard_map/all_to_all | solution.py:76
  541.8 322.1 %all-gather.6.cloned.1.call-start = ((), (), s32[]{:S(2)}) async-start(), calls=%async_computation.8 | async-start | bytes 7372800 | tf_op jit(solution)/shard_map/all_gather | solution.py:97
  596.7 236.3 %all-to-all-start.5 = ((bf16[2,8,72,2048]{2,1,0,3:T(8,128)(2,1)}), bf16[2,8,72,2048]{2,1,0,3:T(8,128)(2,1)}, u32[]{:S(2)}, u32[]{:S(2)}) async-start(bf16[2,8,72,2048]{2,1,0,3:T(8,128)(2,1)} %copy.130), calls=%async_computation.5 | async-start | bytes 16777216 | tf_op jit(solution)/shard_map/all_to_all | solution.py:92
  602.3 5.1 copy-start.7
  602.3 324.6 %all-reduce.2.cloned.1.call-start = ((), (), s32[]{:S(2)}) async-start(), calls=%async_computation.6 | async-start | bytes 262144 | tf_op jit(solution)/shard_map/psum | solution.py:85
  863.9 64.6 %copy-start.1 = (bf16[128,2048]{1,0:T(8,128)(2,1)S(1)}, bf16[128,2048]{1,0:T(8,128)(2,1)}, u32[]{:S(2)}) copy-start(bf16[128,2048]{1,0:T(8,128)(2,1)} %param.13) | copy-start | bytes 1572868
  (4 other events, 11.9 us)
Sparse Core Ops, SparseCore 0:
  113.1 110.4 all-gather.7
  274.7 221.0 all-gather.3
  544.3 178.8 all-gather.5
Sparse Core Ops, SparseCore 1:
  608.9 318.0 all-reduce.1
where the time goes:
time: 946 us; the launch traced here: 936 us
  waiting for transfers between devices  606 us (64%)
  local copies, waits for them, and re-layouts  132 us (14%)
  matrix products  79 us (8%)
  blocking collectives  59.9 us (6%)
  starting transfers between devices  26.6 us (3%)
  other arithmetic  17 us (2%)
  between operations  16.1 us (2%)
    all_to_all x1, waiting for transfers between devices, body(): lax.all_to_all(arrived4, 'dp', split_axis=3, concat_axis=1, tiled=True)  240 us
    all_to_all x1, waiting for transfers between devices, body(): lax.all_to_all(grad_in4, 'dp', split_axis=3, concat_axis=1, tiled=True)  185 us
    all_to_all x1, blocking collectives, body(): lax.all_to_all(send, 'expert', split_axis=1, concat_axis=1, tiled=True)  59.9 us
    psum x1, waiting for transfers between devices, body(): lax.psum(jnp.dot(tokens.T, logit_grad, preferred_element_type=f32), ('exp...  53.9 us
    all_to_all x1, waiting for transfers between devices, body(): lax.all_to_all(grad_send, 'expert', split_axis=1, concat_axis=1, tiled=True)  43.1 us
    all_to_all x1, waiting for transfers between devices, body(): lax.all_to_all(input_grad, 'expert', split_axis=1, concat_axis=1, tiled=T...  42.3 us
    all_to_all x1, waiting for transfers between devices, body(): lax.all_to_all(expert_out, 'expert', split_axis=1, concat_axis=1, tiled=T...  40.4 us
  transfers between devices with their start and end apart: 9, of which 6 were waited for; matrix products, arithmetic and copies ran while one was open for 20% of the time, Pallas kernels for 0%

commit v1 on v0

--- a/solution.py
+++ b/solution.py
@@ -2,6 +2,13 @@
 import jax.numpy as jnp
 from jax import lax
 from jax.sharding import PartitionSpec as P
+
+
+def swap_blocks(value, axis, split, join):
+    peers = lax.axis_size(axis)
+    blocks = jnp.stack(jnp.split(value, peers, axis=split), axis=0)
+    blocks = lax.all_to_all(blocks, axis, split_axis=0, concat_axis=0)
+    return jnp.concatenate(blocks, axis=join)
 
 
 def flat_rows(array):
@@ -89,7 +96,7 @@
     arrived4 = results[2]
     columns = (
         lax.all_to_all(arrived4, "dp", split_axis=3, concat_axis=1, tiled=True),
-        lax.all_to_all(grad_in4, "dp", split_axis=3, concat_axis=1, tiled=True),
+        swap_blocks(grad_in4, "dp", 3, 1),
     )
     hid_shape = (local_experts, groups, capacity, hidden_width)
     hiddens = (

time: 946 us -> 866 us (0.915)
  waiting for transfers between devices: 606 us -> 541 us
  local copies, waits for them, and re-layouts: 132 us -> 115 us
    all_to_all x1, waiting for transfers between devices: 185 us -> 107 us  [swap_blocks(): blocks = lax.all_to_all(blocks, axis, split_axis=0, concat_axis=0)]
    all_to_all x1 -> x0, local copies, waits for them, and re-layouts: 13.3 us -> none  [body(): lax.all_to_all(grad_in4, 'dp', split_axis=3, concat_axis=1, tiled=True)]
    all_to_all x2 -> x1, local copies, waits for them, and re-layouts: 14.7 us -> 2.87 us  [body(): lax.all_to_all(grad_send, 'expert', split_axis=1, concat_axis=1, tiled=True)]
where the time goes in v1:
time: 866 us; the launch traced here: 857 us
  waiting for transfers between devices  541 us (62%)
  local copies, waits for them, and re-layouts  115 us (13%)
  matrix products  79.3 us (9%)
  blocking collectives  59.9 us (7%)
  starting transfers between devices  26 us (3%)
  other arithmetic  19.5 us (2%)
  between operations  16.1 us (2%)
    all_to_all x1, waiting for transfers between devices, body(): lax.all_to_all(arrived4, 'dp', split_axis=3, concat_axis=1, tiled=True)  240 us
    all_to_all x1, waiting for transfers between devices, swap_blocks(): blocks = lax.all_to_all(blocks, axis, split_axis=0, concat_axis=0)  107 us
    psum x1, waiting for transfers between devices, body(): lax.psum(jnp.dot(tokens.T, logit_grad, preferred_element_type=f32), ('exp...  60.9 us
    all_to_all x1, blocking collectives, body(): lax.all_to_all(send, 'expert', split_axis=1, concat_axis=1, tiled=True)  59.9 us
    all_to_all x1, waiting for transfers between devices, body(): lax.all_to_all(input_grad, 'expert', split_axis=1, concat_axis=1, tiled=T...  49 us
    all_to_all x1, waiting for transfers between devices, body(): lax.all_to_all(grad_send, 'expert', split_axis=1, concat_axis=1, tiled=True)  43 us
    all_to_all x1, waiting for transfers between devices, body(): lax.all_to_all(expert_out, 'expert', split_axis=1, concat_axis=1, tiled=T...  40.3 us
  transfers between devices with their start and end apart: 9, of which 6 were waited for; matrix products, arithmetic and copies ran while one was open for 20% of the time, Pallas kernels for 0%

profile of v1, /device:TPU:0, one launch (start us, length us, event | category | flops | bytes accessed | tf_op | source)
XLA Modules:
  0.0 856.6 jit_solution(11295224474678694467)
XLA Ops:
  18.7 6.0 gather_fusion
  27.4 59.9 %all_to_all.40 = bf16[2,8,72,2048]{3,2,0,1:T(8,128)(2,1)S(1)} all-to-all(bf16[2,8,72,2048]{3,2,0,1:T(8,128)(2,1)S(1)} %copy_select_fusion), channel_id=1, replica_groups=mesh['expert'=8,'dp'=4] {'expert'}, dimensions={1} | all-to-all | bytes 9437184 | tf_op jit(solution)/shard_map/all_to_all | solution.py:47
  93.6 5.7 multiply_convert_fusion.2
  111.9 7.0 gather_fusion.5
  119.1 6.0 gather_fusion.3
  125.1 40.3 %all-to-all-done.1 = bf16[2,8,72,2048]{3,2,0,1:T(8,128)(2,1)} async-done(((bf16[2,8,72,2048]{3,2,0,1:T(8,128)(2,1)}), bf16[2,8,72,2048]{3,2,0,1:T(8,128)(2,1)}, u32[]{:S(2)}, u32[]{:S(2)}) %all-to-all-start.1) | async-done | bytes 4718624 | tf_op jit(solution)/shard_map/all_to_all | solution.py:60
  170.6 11.8 %gather_fusion.1 = bf16[1024,2048]{1,0:T(8,128)(2,1)} fusion(bf16[1152,2048]{1,0:T(8,128)(2,1)} %bitcast.110, s32[1024]{0:T(1024)S(1)} %broadcast_clamp_fusion), kind=kCustom, calls=%fused_computation.1 | custom fusion | bytes 8392704 | tf_op jit(solution)/shard_map/gather | solution.py:63
  201.3 11.7 %copy.123 = bf16[2,8,72,2048]{2,1,0,3:T(8,128)(2,1)} copy(bf16[2,8,72,2048]{3,2,0,1:T(8,128)(2,1)} %copy-done.3) | data formatting | bytes 9437184 | tf_op jit(solution)/shard_map/all_to_all | solution.py:47
  213.0 43.0 %all-to-all-done.2 = bf16[2,8,72,2048]{3,2,0,1:T(8,128)(2,1)} async-done(((bf16[2,8,72,2048]{3,2,0,1:T(8,128)(2,1)}), bf16[2,8,72,2048]{3,2,0,1:T(8,128)(2,1)}, u32[]{:S(2)}, u32[]{:S(2)}) %all-to-all-start.2) | async-done | bytes 4718624 | tf_op jit(solution)/shard_map/all_to_all | solution.py:69
  256.1 5.6 all-to-all-start.4
  266.1 8.5 multiply_convert_fusion
  274.6 11.3 %fusion.34 = f32[2,576,2048]{2,1,0:T(8,128)} fusion(bf16[2,576,640]{2,1,0:T(8,128)(2,1)} %get-tuple-element.11, bf16[2,2048,640]{2,1,0:T(8,128)(2,1)} %param.10), kind=kOutput, calls=%fused_computation.91 | convolution fusion | flops 3019898880 | bytes 16154624 | tf_op jit(solution)/shard_map/jrf,jdf->jrd/dot_general | solution.py:79
  285.9 8.1 add_convert_fusion
  296.5 240.4 %all-to-all-done.4 = bf16[2,8,72,2048]{2,1,0,3:T(8,128)(2,1)} async-done(((bf16[2,8,72,2048]{2,1,0,3:T(8,128)(2,1)}), bf16[2,8,72,2048]{2,1,0,3:T(8,128)(2,1)}, u32[]{:S(2)}, u32[]{:S(2)}) %all-to-all-start.4) | async-done | bytes 4718624 | tf_op jit(solution)/shard_map/all_to_all | solution.py:98
  547.7 49.0 %all-to-all-done.3 = bf16[2,8,72,2048]{3,2,0,1:T(8,128)(2,1)} async-done(((bf16[2,8,72,2048]{3,2,0,1:T(8,128)(2,1)}), bf16[2,8,72,2048]{3,2,0,1:T(8,128)(2,1)}, u32[]{:S(2)}, u32[]{:S(2)}) %all-to-all-start.3) | async-done | bytes 4718624 | tf_op jit(solution)/shard_map/all_to_all | solution.py:83
  608.0 10.7 %copy.139 = bf16[2,8,72,4,512]{4,3,2,1,0:T(4,128)(2,1)} copy(bf16[2,8,72,4,512]{2,1,0,4,3:T(8,128)(2,1)} %bitcast.23) | data formatting | bytes 9437184 | tf_op jit(solution)/shard_map/all_to_all | solution.py:98
  618.7 5.6 copy.125
  624.3 5.3 copy.121
  629.6 12.0 %gather_fusion.4 = bf16[1024,2048]{1,0:T(8,128)(2,1)} fusion(bf16[1152,2048]{1,0:T(8,128)(2,1)} %bitcast.109, s32[1024]{0:T(1024)S(1)} %broadcast_clamp_fusion), kind=kCustom, calls=%fused_computation.4 | custom fusion | bytes 8392704 | tf_op jit(solution)/shard_map/gather | solution.py:86
  647.7 106.7 %all-to-all-done.5 = bf16[4,2,8,72,512]{4,3,1,2,0:T(8,128)(2,1)} async-done(((bf16[4,2,8,72,512]{4,3,1,2,0:T(8,128)(2,1)}), bf16[4,2,8,72,512]{4,3,1,2,0:T(8,128)(2,1)}, u32[]{:S(2)}, u32[]{:S(2)}) %all-to-all-start.5) | async-done | bytes 4718624 | tf_op jit(solution)/shard_map/all_to_all | solution.py:10
  759.5 8.4 convolution_convert_fusion.1
  767.8 9.1 %convolution_convert_fusion.3 = bf16[2,512,640]{2,1,0:T(8,128)(2,1)} fusion(bf16[2,2304,512]{2,1,0:T(8,128)(2,1)} %bitcast.114, bf16[2,2304,640]{2,1,0:T(8,128)(2,1)} %bitcast.135), kind=kOutput, calls=%fused_computation.29 | convolution fusion | flops 3020554240 | bytes 11927552 | tf_op jit(solution)/shard_map/jrd,jrf->jdf/dot_general | solution.py:109
  777.0 9.5 %convolution_convert_fusion.2 = bf16[2,512,640]{2,1,0:T(8,128)(2,1)} fusion(bf16[2,2304,512]{2,1,0:T(8,128)(2,1)} %bitcast.115, bf16[2,2304,640]{2,1,0:T(8,128)(2,1)} %bitcast.136), kind=kOutput, calls=%fused_computation.28 | convolution fusion | flops 3020554240 | bytes 11927552 | tf_op jit(solution)/shard_map/jrd,jrf->jdf/dot_general | solution.py:112
  786.4 60.9 %all-reduce.2.cloned.1.call-done = f32[2048,16]{0,1:T(8,128)} async-done(((f32[2048,16]{0,1:T(8,128)}), f32[2048,16]{0,1:T(8,128)}) %all-reduce.2.cloned.1.call-update) | async-done | bytes 131088 | tf_op jit(solution)/shard_map/psum | solution.py:92
  (115 shorter events, 98.0 us)
Async XLA Ops:
  8.0 111.1 %copy-start = (bf16[128,2048]{1,0:T(8,128)(2,1)S(1)}, bf16[128,2048]{1,0:T(8,128)(2,1)}, u32[]{:S(2)}) copy-start(bf16[128,2048]{1,0:T(8,128)(2,1)} %param.13) | copy-start | bytes 1572868
  8.0 10.7 %copy-start.2 = (bf16[128,2048]{1,0:T(8,128)(2,1)S(1)}, bf16[128,2048]{1,0:T(8,128)(2,1)}, u32[]{:S(2)}) copy-start(bf16[128,2048]{1,0:T(8,128)(2,1)} %param.7) | copy-start | bytes 1572868
  8.9 15.8 %copy-start.6 = (s32[128,8]{1,0:T(8,128)}, s32[128,8]{1,0:T(8,128)S(1)}, u32[]{:S(2)}) copy-start(s32[128,8]{1,0:T(8,128)S(1)} %copy.106) | copy-start | bytes 12292
  27.4 62.3 %slice-start.2 = ((s8[5242880]{0:T(1024)(128)(4,1)}), s8[4194304]{0:T(1024)(128)(4,1)S(1)}, s32[]{:S(2)}) async-start(s8[5242880]{0:T(1024)(128)(4,1)} %bitcast.139), calls=%async_computation.12 | async-start | bytes 8388608
  87.3 6.3 slice-start.4
  89.8 9.6 %slice-start = ((s8[5242880]{0:T(1024)(128)(4,1)}), s8[4194304]{0:T(1024)(128)(4,1)S(1)}, s32[]{:S(2)}) async-start(s8[5242880]{0:T(1024)(128)(4,1)} %bitcast.137), calls=%async_computation.10 | async-start | bytes 8388608
  93.6 5.7 copy-start.10
  93.6 5.7 slice-start.1
  99.3 4.1 copy-start.4
  105.9 5.5 copy-start.9
  105.9 5.7 copy-start.8
  105.9 59.5 %all-to-all-start.1 = ((bf16[2,8,72,2048]{3,2,0,1:T(8,128)(2,1)}), bf16[2,8,72,2048]{3,2,0,1:T(8,128)(2,1)}, u32[]{:S(2)}, u32[]{:S(2)}) async-start(bf16[2,8,72,2048]{3,2,0,1:T(8,128)(2,1)} %copy.114), calls=%async_computation.1 | async-start | bytes 9437184 | tf_op jit(solution)/shard_map/all_to_all | solution.py:60
  110.7 648.8 %all-gather.8.cloned.1.call-start = ((), (), s32[]{:S(2)}) async-start(), calls=%async_computation.9 | async-start | bytes 7372800 | tf_op jit(solution)/shard_map/all_gather | solution.py:105
  196.7 59.4 %all-to-all-start.2 = ((bf16[2,8,72,2048]{3,2,0,1:T(8,128)(2,1)}), bf16[2,8,72,2048]{3,2,0,1:T(8,128)(2,1)}, u32[]{:S(2)}, u32[]{:S(2)}) async-start(bf16[2,8,72,2048]{3,2,0,1:T(8,128)(2,1)} %fusion.1), calls=%async_computation.2 | async-start | bytes 9437184 | tf_op jit(solution)/shard_map/all_to_all | solution.py:69
  256.1 280.8 %all-to-all-start.4 = ((bf16[2,8,72,2048]{2,1,0,3:T(8,128)(2,1)}), bf16[2,8,72,2048]{2,1,0,3:T(8,128)(2,1)}, u32[]{:S(2)}, u32[]{:S(2)}) async-start(bf16[2,8,72,2048]{2,1,0,3:T(8,128)(2,1)} %copy.123), calls=%async_computation.4 | async-start | bytes 16777216 | tf_op jit(solution)/shard_map/all_to_all | solution.py:98
  261.7 506.1 %all-gather.4.cloned.1.call-start = ((), (), s32[]{:S(2)}) async-start(), calls=%async_computation.7 | async-start | bytes 7372800 | tf_op jit(solution)/shard_map/all_gather | solution.py:103
  261.9 4.1 copy-start.12
  274.5 11.3 %copy-start.5 = (bf16[2,576,640]{2,1,0:T(8,128)(2,1)}, bf16[2,576,640]{2,1,0:T(8,128)(2,1)S(1)}, u32[]{:S(2)}) copy-start(bf16[2,576,640]{2,1,0:T(8,128)(2,1)S(1)} %get-tuple-element.10) | copy-start | bytes 4423684
  536.9 59.8 %all-to-all-start.3 = ((bf16[2,8,72,2048]{3,2,0,1:T(8,128)(2,1)}), bf16[2,8,72,2048]{3,2,0,1:T(8,128)(2,1)}, u32[]{:S(2)}, u32[]{:S(2)}) async-start(bf16[2,8,72,2048]{3,2,0,1:T(8,128)(2,1)} %copy.120), calls=%async_computation.3 | async-start | bytes 9437184 | tf_op jit(solution)/shard_map/all_to_all | solution.py:83
  541.9 235.1 %all-gather.6.cloned.1.call-start = ((), (), s32[]{:S(2)}) async-start(), calls=%async_computation.8 | async-start | bytes 7372800 | tf_op jit(solution)/shard_map/all_gather | solution.py:104
  596.7 157.7 %all-to-all-start.5 = ((bf16[4,2,8,72,512]{4,3,1,2,0:T(8,128)(2,1)}), bf16[4,2,8,72,512]{4,3,1,2,0:T(8,128)(2,1)}, u32[]{:S(2)}, u32[]{:S(2)}) async-start(bf16[4,2,8,72,512]{4,3,1,2,0:T(8,128)(2,1)} %pad_maximum_fusion), calls=%async_computation.5 | async-start | bytes 9437184 | tf_op jit(solution)/shard_map/all_to_all | solution.py:10
  601.7 5.1 copy-start.7
  601.7 245.7 %all-reduce.2.cloned.1.call-start = ((), (), s32[]{:S(2)}) async-start(), calls=%async_computation.6 | async-start | bytes 262144 | tf_op jit(solution)/shard_map/psum | solution.py:92
  777.0 72.0 %copy-start.1 = (bf16[128,2048]{1,0:T(8,128)(2,1)S(1)}, bf16[128,2048]{1,0:T(8,128)(2,1)}, u32[]{:S(2)}) copy-start(bf16[128,2048]{1,0:T(8,128)(2,1)} %param.13) | copy-start | bytes 1572868
  (4 other events, 11.9 us)
Sparse Core Ops, SparseCore 0:
  113.1 110.4 all-gather.7
  274.7 221.0 all-gather.3
  544.3 184.8 all-gather.5
Sparse Core Ops, SparseCore 1:
  608.3 239.0 all-reduce.1
